TPU v7x, 512 devices: a whole 4x4x16 slice. The times are simulated.
512 devices in a mesh: mp: 2 (over y_hi), tok: 8 (over x, core), lat: 32 (over z, y_lo).
Axes of the slice: x: 4, y: 4 (y_hi: 2, y_lo: 2; y = y_hi * 2 + y_lo), z: 16, core: 2. Of those that a mesh axis runs over, the one named last changes fastest.
Arguments:
- inputs: bfloat16 [2, 384, 4608], P('mp', 'lat', 'tok'), may hold values from -6 to 6
- gate_w: bfloat16 [2, 4608, 18432], P('mp', 'tok', 'lat'), may hold values from -0.09375 to 0.09375
- up_w: bfloat16 [2, 4608, 18432], P('mp', 'tok', 'lat'), may hold values from -0.09375 to 0.09375
- down_w: bfloat16 [2, 18432, 4608], P('mp', 'lat', 'tok'), may hold values from -0.046875 to 0.046875
- enc_w: bfloat16 [2, 4608, 8192], P('mp', 'tok', 'lat'), may hold values from -0.0625 to 0.0625
- enc_bias: float32 [8192], P('lat'), may hold values from -3 to 3
- dec_w: bfloat16 [8192, 2, 4608], P('lat', 'mp', 'tok'), may hold values from -0.0625 to 0.0625
- dec_bias: float32 [2, 4608], P('mp', 'tok'), may hold values from -3 to 3
Outputs:
- recon_error: float32 [2, 384, 4608], P('mp', 'lat', 'tok')
- dec_grad: float32 [8192, 2, 4608], P('lat', 'mp', 'tok')
- latent_grad: float32 [384, 8192], P(None, 'lat')
All inputs are finite; a program needn't handle non-finite values.
Results may differ from a plain program's by a relative error of at most 0.009.
Values may be sent and summed in bfloat16 or wider, within the bound.
A program may use at most 64 MiB of HBM per device.

v0:
```python
import jax
import jax.numpy as jnp
from jax import lax
from jax.sharding import PartitionSpec as P


def contract_rows(left, right):
    return lax.dot_general(
        left, right, (((0,), (0,)), ((), ())), preferred_element_type=jnp.float32
    )


def contract_cols(left, right):
    return lax.dot_general(
        left, right, (((1,), (1,)), ((), ())), preferred_element_type=jnp.float32
    )


def body(inputs, gate_w, up_w, down_w, enc_w, enc_bias, dec_w, dec_bias):
    x_rows = inputs[0]
    gathered = lax.all_gather(x_rows, "lat", axis=0, tiled=True)
    gate_local = gate_w[0]
    up_local = up_w[0]
    width = gate_local.shape[1]
    block = gathered
    both = lax.psum_scatter(
        jnp.concatenate(
            [
                jnp.dot(block, gate_local, preferred_element_type=jnp.float32),
                jnp.dot(block, up_local, preferred_element_type=jnp.float32),
            ],
            axis=1,
        ),
        "tok",
        scatter_dimension=0,
        tiled=True,
    )
    hidden = (jax.nn.gelu(both[:, :width], approximate=True) * both[:, width:]).astype(jnp.bfloat16)
    hidden_all = lax.all_gather(hidden, "tok", axis=0, tiled=True)
    down_local = down_w[0]
    block = hidden_all
    acts = lax.psum_scatter(
        jnp.dot(block, down_local, preferred_element_type=jnp.float32),
        "lat",
        scatter_dimension=0,
        tiled=True,
    ).astype(jnp.bfloat16)
    acts_all = lax.all_gather(acts, "lat", axis=0, tiled=True)
    partial_pre = jnp.dot(acts_all, enc_w[0], preferred_element_type=jnp.float32)
    pre = lax.psum(partial_pre, ("mp", "tok"))
    codes = jnp.maximum(pre + enc_bias, 0.0).astype(jnp.bfloat16)
    decoder = dec_w[:, 0, :]
    bias_row = dec_bias[0]
    block = codes
    recon = lax.psum_scatter(
        jnp.dot(block, decoder, preferred_element_type=jnp.float32),
        "lat",
        scatter_dimension=0,
        tiled=True,
    )
    error = recon + bias_row - acts.astype(jnp.float32)
    error_all = lax.all_gather(error.astype(jnp.bfloat16), "lat", axis=0, tiled=True)
    decoder_grad = contract_rows(codes, error_all)
    latent_grad = lax.psum(contract_cols(error_all, decoder), ("mp", "tok"))
    return (error[None], decoder_grad[:, None, :], latent_grad)


def solution(mesh):
    in_specs = (
        P("mp", "lat", "tok"),
        P("mp", "tok", "lat"),
        P("mp", "tok", "lat"),
        P("mp", "lat", "tok"),
        P("mp", "tok", "lat"),
        P("lat"),
        P("lat", "mp", "tok"),
        P("mp", "tok"),
    )
    out_specs = (P("mp", "lat", "tok"), P("lat", "mp", "tok"), P(None, "lat"))
    return jax.shard_map(body, mesh=mesh, in_specs=in_specs, out_specs=out_specs, check_vma=False)
```

profile of v0, /device:TPU:1, one launch (start us, length us, event | category | flops | bytes accessed | tf_op | source)
XLA Modules:
  0.0 789.7 jit_solution(4947730989583786598)
XLA Ops:
  8.0 61.9 %all-gather = bf16[1,384,576]{2,0,1:T(2,128)(2,1)S(1)} all-gather(bf16[1,12,576]{2,0,1:T(2,128)(2,1)S(1)} %copy.20), channel_id=2, replica_groups=mesh['mp'=2,'tok'=8,'lat'=32] {'lat'}, dimensions={1}, use_global_device_ids=true | all-gather | bytes 456192 | tf_op jit(solution)/shard_map/all_gather | solution.py:21
  72.1 2.0 copy.25
  74.1 47.7 %reduce-scatter.8.cloned.1.call-done = f32[48,1152]{1,0:T(8,128)} async-done(((f32[384,1152]{1,0:T(8,128)}), f32[48,1152]{1,0:T(8,128)}) %reduce-scatter.8.cloned.1.call-update) | async-done | bytes 221200 | tf_op jit(solution)/shard_map/reduce_scatter | solution.py:26
  121.8 1.1 fusion.24
  122.9 15.4 %all_gather.13 = bf16[384,576]{1,0:T(8,128)(2,1)S(1)} all-gather(bf16[48,576]{1,0:T(8,128)(2,1)S(1)} %fusion.24), channel_id=1, replica_groups=mesh['mp'=2,'tok'=8,'lat'=32] {'tok'}, dimensions={0}, use_global_device_ids=true | all-gather | bytes 497664 | tf_op jit(solution)/shard_map/all_gather | solution.py:39
  138.8 59.0 %fusion = f32[16,576]{1,0:T(8,128)S(1)} fusion(f32[384,576]{1,0:T(8,128)S(1)} %fusion.2), kind=kCustom, calls=%all-reduce-scatter | all-reduce-scatter fusion | flops 294913 | bytes 923648
  197.9 1.7 collective-permute-start
  199.6 2.1 collective-permute-start.1
  201.7 6.0 collective-permute-start.7
  207.7 4.9 collective-permute-start.2
  212.7 4.9 collective-permute-start.3
  217.6 2.1 collective-permute-start.4
  219.8 3.5 collective-permute-start.5
  223.2 2.8 collective-permute-start.6
  226.1 1.3 dynamic-slice.6
  228.1 1.3 concatenate.4
  229.4 49.4 %all-gather.1 = bf16[32,12,576]{2,1,0:T(8,128)(2,1)S(1)} all-gather(bf16[1,12,576]{2,1,0:T(8,128)(2,1)S(1)} %fusion.31), channel_id=1, replica_groups=mesh['mp'=2,'tok'=8,'lat'=32] {'lat'}, dimensions={0}, use_global_device_ids=true | all-gather | bytes 456192 | tf_op jit(solution)/shard_map/all_gather | solution.py:48
  280.2 180.0 %all-reduce.7.cloned.1.call-done = f32[384,256]{1,0:T(8,128)} async-done(((f32[384,256]{1,0:T(8,128)}), f32[384,256]{1,0:T(8,128)}) %all-reduce.7.cloned.1.call-update) | async-done | bytes 393232 | tf_op jit(solution)/shard_map/psum | solution.py:50
  460.2 1.3 fusion.12
  461.6 59.2 %fusion.1 = f32[16,576]{1,0:T(8,128)S(1)} fusion(f32[384,576]{1,0:T(8,128)S(1)} %fusion.12), kind=kCustom, calls=%all-reduce-scatter.1 | all-reduce-scatter fusion | flops 294913 | bytes 923648
  520.7 1.3 collective-permute-start.10
  522.0 3.4 collective-permute-start.11
  525.5 7.0 collective-permute-start.15
  532.6 4.5 collective-permute-start.12
  537.1 3.9 collective-permute-start.13
  541.0 2.9 collective-permute-start.14
  543.9 3.1 collective-permute-start.8
  547.0 2.2 collective-permute-start.9
  551.3 48.9 %all-gather.2 = bf16[32,12,576]{2,1,0:T(8,128)(2,1)S(1)} all-gather(bf16[1,12,576]{2,1,0:T(8,128)(2,1)S(1)} %get-tuple-element.18), channel_id=1, replica_groups=mesh['mp'=2,'tok'=8,'lat'=32] {'lat'}, dimensions={0}, use_global_device_ids=true | all-gather | bytes 456192 | tf_op jit(solution)/shard_map/all_gather | solution.py:62
  602.2 1.2 convolution_bitcast_fusion
  603.3 178.1 %all-reduce.9.cloned.1.call-done = f32[384,256]{1,0:T(8,128)} async-done(((f32[384,256]{1,0:T(8,128)}), f32[384,256]{1,0:T(8,128)}) %all-reduce.9.cloned.1.call-update) | async-done | bytes 393232 | tf_op jit(solution)/shard_map/psum | solution.py:64
  781.4 1.8 copy.29
  (56 shorter events, 9.1 us)
Async XLA Ops:
  7.2 63.5 %copy-start = (bf16[1,576,576]{2,1,0:T(8,128)(2,1)S(1)}, bf16[1,576,576]{2,1,0:T(8,128)(2,1)}, u32[]{:S(2)}) copy-start(bf16[1,576,576]{2,1,0:T(8,128)(2,1)} %param.10) | copy-start | bytes 1990660
  7.2 114.6 %reduce-scatter.8.cloned.1.call-start = ((), (), s32[]{:S(2)}) async-start(), calls=%async_computation.3 | async-start | bytes 1990656 | tf_op jit(solution)/shard_map/reduce_scatter | solution.py:26
  70.0 1.3 copy-start.3
  74.0 64.2 %copy-start.4 = (bf16[1,576,576]{2,1,0:T(8,128)(2,1)S(1)}, bf16[1,576,576]{2,1,0:T(8,128)(2,1)}, u32[]{:S(2)}) copy-start(bf16[1,576,576]{2,1,0:T(8,128)(2,1)} %param.11) | copy-start | bytes 1990660
  74.1 386.2 %all-reduce.7.cloned.1.call-start = ((), (), s32[]{:S(2)}) async-start(), calls=%async_computation.1 | async-start | bytes 786432 | tf_op jit(solution)/shard_map/psum | solution.py:50
  138.8 140.3 %copy-start.5 = (bf16[1,576,256]{2,1,0:T(8,128)(2,1)S(1)}, bf16[1,576,256]{2,1,0:T(8,128)(2,1)}, u32[]{:S(2)}) copy-start(bf16[1,576,256]{2,1,0:T(8,128)(2,1)} %param.12) | copy-start | bytes 884740
  197.9 21.9 %collective-permute-start = (bf16[16,576]{1,0:T(8,128)(2,1)S(1)}, bf16[16,576]{1,0:T(8,128)(2,1)S(1)}, u32[]{:S(2)}, u32[]{:S(2)}) collective-permute-start(bf16[16,576]{1,0:T(8,128)(2,1)S(1)} %convert.14), channel_id=1, source_target_pairs={{0,1},{1,2},{2,3},{3,4},{4,5},{5,6},{6,7},{7,8},{8,9},{9,10},{10,1... | collective-permute-start | bytes 55304
  199.6 23.6 %collective-permute-start.1 = (bf16[16,576]{1,0:T(8,128)(2,1)S(1)}, bf16[16,576]{1,0:T(8,128)(2,1)S(1)}, u32[]{:S(2)}, u32[]{:S(2)}) collective-permute-start(bf16[16,576]{1,0:T(8,128)(2,1)S(1)} %convert.14), channel_id=1, source_target_pairs={{0,2},{1,3},{2,4},{3,5},{4,6},{5,7},{6,8},{7,9},{8,10},{9,11},{10,... | collective-permute-start | bytes 55304
  201.7 15.9 %collective-permute-start.7 = (bf16[12,576]{1,0:T(8,128)(2,1)S(1)}, bf16[12,576]{1,0:T(8,128)(2,1)S(1)}, u32[]{:S(2)}, u32[]{:S(2)}) collective-permute-start(bf16[12,576]{1,0:T(8,128)(2,1)S(1)} %slice.10), channel_id=1, source_target_pairs={{0,8},{1,9},{2,10},{3,11},{4,12},{5,13},{6,14},{7,15},{8,16},{9,17... | collective-permute-start | bytes 41480
  207.7 20.3 %collective-permute-start.2 = (bf16[16,576]{1,0:T(8,128)(2,1)S(1)}, bf16[16,576]{1,0:T(8,128)(2,1)S(1)}, u32[]{:S(2)}, u32[]{:S(2)}) collective-permute-start(bf16[16,576]{1,0:T(8,128)(2,1)S(1)} %convert.14), channel_id=1, source_target_pairs={{0,3},{1,4},{2,5},{3,6},{4,7},{5,8},{6,9},{7,10},{8,11},{9,12},{10... | collective-permute-start | bytes 55304
  212.7 15.3 %collective-permute-start.3 = (bf16[16,576]{1,0:T(8,128)(2,1)S(1)}, bf16[16,576]{1,0:T(8,128)(2,1)S(1)}, u32[]{:S(2)}, u32[]{:S(2)}) collective-permute-start(bf16[16,576]{1,0:T(8,128)(2,1)S(1)} %convert.14), channel_id=1, source_target_pairs={{0,4},{1,5},{2,6},{3,7},{4,8},{5,9},{6,10},{7,11},{8,12},{9,13},{1... | collective-permute-start | bytes 55304
  217.6 10.4 %collective-permute-start.4 = (bf16[16,576]{1,0:T(8,128)(2,1)S(1)}, bf16[16,576]{1,0:T(8,128)(2,1)S(1)}, u32[]{:S(2)}, u32[]{:S(2)}) collective-permute-start(bf16[16,576]{1,0:T(8,128)(2,1)S(1)} %convert.14), channel_id=1, source_target_pairs={{0,5},{1,6},{2,7},{3,8},{4,9},{5,10},{6,11},{7,12},{8,13},{9,14},{... | collective-permute-start | bytes 55304
  219.8 8.3 %collective-permute-start.5 = (bf16[16,576]{1,0:T(8,128)(2,1)S(1)}, bf16[16,576]{1,0:T(8,128)(2,1)S(1)}, u32[]{:S(2)}, u32[]{:S(2)}) collective-permute-start(bf16[16,576]{1,0:T(8,128)(2,1)S(1)} %convert.14), channel_id=1, source_target_pairs={{0,6},{1,7},{2,8},{3,9},{4,10},{5,11},{6,12},{7,13},{8,14},{9,15},... | collective-permute-start | bytes 55304
  223.2 4.8 collective-permute-start.6
  229.4 230.8 %copy-start.2 = (bf16[256,1,576]{0,2,1:T(8,128)(2,1)S(1)}, bf16[256,1,576]{0,2,1:T(8,128)(2,1)}, u32[]{:S(2)}) copy-start(bf16[256,1,576]{0,2,1:T(8,128)(2,1)} %param.14) | copy-start | bytes 884740
  229.4 230.8 %copy-start.6 = (f32[256]{0:T(256)S(1)}, f32[256]{0:T(256)}, u32[]{:S(2)}) copy-start(f32[256]{0:T(256)} %param.13) | copy-start | bytes 3076
  280.2 269.0 %copy-start.7 = (f32[1,576]{1,0:T(1,128)S(1)}, f32[1,576]{1,0:T(1,128)}, u32[]{:S(2)}) copy-start(f32[1,576]{1,0:T(1,128)} %param.15) | copy-start | bytes 6916
  280.2 501.2 %all-reduce.9.cloned.1.call-start = ((), (), s32[]{:S(2)}) async-start(), calls=%async_computation.2 | async-start | bytes 786432 | tf_op jit(solution)/shard_map/psum | solution.py:64
  520.7 23.1 %collective-permute-start.10 = (f32[16,576]{1,0:T(8,128)S(1)}, f32[16,576]{1,0:T(8,128)S(1)}, u32[]{:S(2)}, u32[]{:S(2)}) collective-permute-start(f32[16,576]{1,0:T(8,128)S(1)} %fusion.1), channel_id=1, source_target_pairs={{0,3},{1,4},{2,5},{3,6},{4,7},{5,8},{6,9},{7,10},{8,11},{9,12},{10... | collective-permute-start | bytes 110600
  522.0 24.9 %collective-permute-start.11 = (f32[16,576]{1,0:T(8,128)S(1)}, f32[16,576]{1,0:T(8,128)S(1)}, u32[]{:S(2)}, u32[]{:S(2)}) collective-permute-start(f32[16,576]{1,0:T(8,128)S(1)} %fusion.1), channel_id=1, source_target_pairs={{0,4},{1,5},{2,6},{3,7},{4,8},{5,9},{6,10},{7,11},{8,12},{9,13},{1... | collective-permute-start | bytes 110600
  525.5 15.5 %collective-permute-start.15 = (f32[12,576]{1,0:T(8,128)S(1)}, f32[12,576]{1,0:T(8,128)S(1)}, u32[]{:S(2)}, u32[]{:S(2)}) collective-permute-start(f32[12,576]{1,0:T(8,128)S(1)} %slice.11), channel_id=1, source_target_pairs={{0,8},{1,9},{2,10},{3,11},{4,12},{5,13},{6,14},{7,15},{8,16},{9,17... | collective-permute-start | bytes 82952
  532.6 16.7 %collective-permute-start.12 = (f32[16,576]{1,0:T(8,128)S(1)}, f32[16,576]{1,0:T(8,128)S(1)}, u32[]{:S(2)}, u32[]{:S(2)}) collective-permute-start(f32[16,576]{1,0:T(8,128)S(1)} %fusion.1), channel_id=1, source_target_pairs={{0,5},{1,6},{2,7},{3,8},{4,9},{5,10},{6,11},{7,12},{8,13},{9,14},{... | collective-permute-start | bytes 110600
  537.1 12.2 %collective-permute-start.13 = (f32[16,576]{1,0:T(8,128)S(1)}, f32[16,576]{1,0:T(8,128)S(1)}, u32[]{:S(2)}, u32[]{:S(2)}) collective-permute-start(f32[16,576]{1,0:T(8,128)S(1)} %fusion.1), channel_id=1, source_target_pairs={{0,6},{1,7},{2,8},{3,9},{4,10},{5,11},{6,12},{7,13},{8,14},{9,15},... | collective-permute-start | bytes 110600
  541.0 8.2 %collective-permute-start.14 = (f32[16,576]{1,0:T(8,128)S(1)}, f32[16,576]{1,0:T(8,128)S(1)}, u32[]{:S(2)}, u32[]{:S(2)}) collective-permute-start(f32[16,576]{1,0:T(8,128)S(1)} %fusion.1), channel_id=1, source_target_pairs={{0,7},{1,8},{2,9},{3,10},{4,11},{5,12},{6,13},{7,14},{8,15},{9,16}... | collective-permute-start | bytes 110600
  543.9 5.4 collective-permute-start.8
  547.0 3.3 collective-permute-start.9
  551.3 50.8 %copy-start.1 = (f32[384,256]{1,0:T(8,128)S(1)}, f32[384,256]{1,0:T(8,128)}, u32[]{:S(2)}) copy-start(f32[384,256]{1,0:T(8,128)} %all-reduce.7.cloned.1.call-done) | copy-start | bytes 1179652
Sparse Core Ops, SparseCore 0:
  74.2 47.5 reduce-scatter.7
  280.3 179.8 all-reduce.6
  601.6 179.7 all-reduce.8
where the time goes:
time: 790 us
  waiting for transfers between devices  407 us (52%)
  blocking collectives  294 us (37%)
  starting transfers between devices  56.6 us (7%)
  between operations  14.9 us (2%)
  local copies, waits for them, and re-layouts  10 us (1%)
    psum x1, waiting for transfers between devices, body(): pre = lax.psum(partial_pre, ('mp', 'tok'))  180 us
    psum x1, waiting for transfers between devices, body(): latent_grad = lax.psum(contract_cols(error_all, decoder), ('mp', 'tok'))  178 us
    unnamed x2, blocking collectives  118 us
    all_gather x1, blocking collectives, body(): gathered = lax.all_gather(x_rows, 'lat', axis=0, tiled=True)  61.9 us
    unnamed x16, starting transfers between devices  56.5 us
    all_gather x1, blocking collectives, body(): acts_all = lax.all_gather(acts, 'lat', axis=0, tiled=True)  49.4 us
    all_gather x1, blocking collectives, body(): lax.all_gather(error.astype(jnp.bfloat16), 'lat', axis=0, tiled=True)  48.9 us
    reduce_scatter x1, waiting for transfers between devices, body(): lax.psum_scatter(jnp.concatenate([jnp.dot(block, gate_local, preferred_el...  47.7 us
  transfers between devices with their start and end apart: 19, of which 4 were waited for; matrix products, arithmetic and copies ran while one was open for 0% of the time, Pallas kernels for 0%

commit v1 on v0

--- a/solution.py
+++ b/solution.py
@@ -61,7 +61,9 @@
     error = recon + bias_row - acts.astype(jnp.float32)
     error_all = lax.all_gather(error.astype(jnp.bfloat16), "lat", axis=0, tiled=True)
     decoder_grad = contract_rows(codes, error_all)
-    latent_grad = lax.psum(contract_cols(error_all, decoder), ("mp", "tok"))
+    latent_grad = jax.lax.psum(
+        jax.lax.psum(contract_cols(error_all, decoder), axis_name="tok"), "mp"
+    )
     return (error[None], decoder_grad[:, None, :], latent_grad)
 
 

time: 790 us -> 764 us (0.967)
  waiting for transfers between devices: 407 us -> 380 us
    psum x1 -> x2, waiting for transfers between devices: 178 us -> 151 us  [the longest x1 101 us: body(): jax.lax.psum(contract_cols(error_all, decoder), axis_name='tok')]
  transfers between devices with their start and end apart: 19 -> 20, of which waited for: 4 -> 5; matrix products, arithmetic and copies ran while one was open for 0% -> 0% of each run, Pallas kernels for 0% -> 0%
where the time goes in v1:
time: 764 us; the launch traced here: 763 us
  waiting for transfers between devices  380 us (50%)
  blocking collectives  294 us (38%)
  starting transfers between devices  56.6 us (7%)
  between operations  14.9 us (2%)
  local copies, waits for them, and re-layouts  10 us (1%)
    psum x1, waiting for transfers between devices, body(): pre = lax.psum(partial_pre, ('mp', 'tok'))  180 us
    unnamed x2, blocking collectives  118 us
    psum x1, waiting for transfers between devices, body(): jax.lax.psum(contract_cols(error_all, decoder), axis_name='tok')  101 us
    all_gather x1, blocking collectives, body(): gathered = lax.all_gather(x_rows, 'lat', axis=0, tiled=True)  61.9 us
    unnamed x16, starting transfers between devices  56.5 us
    psum x1, waiting for transfers between devices, body(): jax.lax.psum(jax.lax.psum(contract_cols(error_all, decoder), axis_name='t...  50.9 us
    all_gather x1, blocking collectives, body(): acts_all = lax.all_gather(acts, 'lat', axis=0, tiled=True)  49.4 us
    all_gather x1, blocking collectives, body(): lax.all_gather(error.astype(jnp.bfloat16), 'lat', axis=0, tiled=True)  48.9 us
  transfers between devices with their start and end apart: 20, of which 5 were waited for; matrix products, arithmetic and copies ran while one was open for 0% of the time, Pallas kernels for 0%

profile of v1, /device:TPU:1, one launch (start us, length us, event | category | flops | bytes accessed | tf_op | source)
XLA Modules:
  0.0 763.2 jit_solution(16426075653769772184)
XLA Ops:
  8.0 61.9 %all-gather = bf16[1,384,576]{2,0,1:T(2,128)(2,1)S(1)} all-gather(bf16[1,12,576]{2,0,1:T(2,128)(2,1)S(1)} %copy.20), channel_id=2, replica_groups=mesh['mp'=2,'tok'=8,'lat'=32] {'lat'}, dimensions={1}, use_global_device_ids=true | all-gather | bytes 456192 | tf_op jit(solution)/shard_map/all_gather | solution.py:21
  72.1 2.0 copy.25
  74.1 47.7 %reduce-scatter.8.cloned.1.call-done = f32[48,1152]{1,0:T(8,128)} async-done(((f32[384,1152]{1,0:T(8,128)}), f32[48,1152]{1,0:T(8,128)}) %reduce-scatter.8.cloned.1.call-update) | async-done | bytes 221200 | tf_op jit(solution)/shard_map/reduce_scatter | solution.py:26
  122.9 15.4 %all_gather.13 = bf16[384,576]{1,0:T(8,128)(2,1)S(1)} all-gather(bf16[48,576]{1,0:T(8,128)(2,1)S(1)} %fusion.24), channel_id=1, replica_groups=mesh['mp'=2,'tok'=8,'lat'=32] {'tok'}, dimensions={0}, use_global_device_ids=true | all-gather | bytes 497664 | tf_op jit(solution)/shard_map/all_gather | solution.py:39
  138.8 59.0 %fusion = f32[16,576]{1,0:T(8,128)S(1)} fusion(f32[384,576]{1,0:T(8,128)S(1)} %fusion.2), kind=kCustom, calls=%all-reduce-scatter | all-reduce-scatter fusion | flops 294913 | bytes 923648
  197.9 1.7 collective-permute-start
  199.6 2.1 collective-permute-start.1
  201.7 6.0 collective-permute-start.7
  207.7 4.9 collective-permute-start.2
  212.7 4.9 collective-permute-start.3
  217.6 2.1 collective-permute-start.4
  219.8 3.5 collective-permute-start.5
  223.2 2.8 collective-permute-start.6
  226.1 1.3 dynamic-slice.6
  228.1 1.3 concatenate.4
  229.4 49.4 %all-gather.1 = bf16[32,12,576]{2,1,0:T(8,128)(2,1)S(1)} all-gather(bf16[1,12,576]{2,1,0:T(8,128)(2,1)S(1)} %fusion.31), channel_id=1, replica_groups=mesh['mp'=2,'tok'=8,'lat'=32] {'lat'}, dimensions={0}, use_global_device_ids=true | all-gather | bytes 456192 | tf_op jit(solution)/shard_map/all_gather | solution.py:48
  280.2 180.0 %all-reduce.8.cloned.1.call-done = f32[384,256]{1,0:T(8,128)} async-done(((f32[384,256]{1,0:T(8,128)}), f32[384,256]{1,0:T(8,128)}) %all-reduce.8.cloned.1.call-update) | async-done | bytes 393232 | tf_op jit(solution)/shard_map/psum | solution.py:50
  460.2 1.3 fusion.12
  461.6 59.2 %fusion.1 = f32[16,576]{1,0:T(8,128)S(1)} fusion(f32[384,576]{1,0:T(8,128)S(1)} %fusion.12), kind=kCustom, calls=%all-reduce-scatter.1 | all-reduce-scatter fusion | flops 294913 | bytes 923648
  520.7 1.3 collective-permute-start.10
  522.0 3.4 collective-permute-start.11
  525.5 7.0 collective-permute-start.15
  532.6 4.5 collective-permute-start.12
  537.1 3.9 collective-permute-start.13
  541.0 2.9 collective-permute-start.14
  543.9 3.1 collective-permute-start.8
  547.0 2.2 collective-permute-start.9
  551.3 48.9 %all-gather.2 = bf16[32,12,576]{2,1,0:T(8,128)(2,1)S(1)} all-gather(bf16[1,12,576]{2,1,0:T(8,128)(2,1)S(1)} %get-tuple-element.18), channel_id=1, replica_groups=mesh['mp'=2,'tok'=8,'lat'=32] {'lat'}, dimensions={0}, use_global_device_ids=true | all-gather | bytes 456192 | tf_op jit(solution)/shard_map/all_gather | solution.py:62
  601.6 100.6 %all-reduce.10.cloned.1.call-done = f32[384,256]{1,0:T(8,128)} async-done(((f32[384,256]{1,0:T(8,128)}), f32[384,256]{1,0:T(8,128)}) %all-reduce.10.cloned.1.call-update) | async-done | bytes 393232 | tf_op jit(solution)/shard_map/psum | solution.py:65
  702.8 1.2 convolution_bitcast_fusion
  704.0 50.9 %all-reduce.12.cloned.1.call-done = f32[384,256]{1,0:T(8,128)} async-done(((f32[384,256]{1,0:T(8,128)}), f32[384,256]{1,0:T(8,128)}) %all-reduce.12.cloned.1.call-update) | async-done | bytes 393232 | tf_op jit(solution)/shard_map/psum | solution.py:64
  754.9 1.8 copy.30
  (59 shorter events, 10.2 us)
Async XLA Ops:
  7.2 63.5 %copy-start = (bf16[1,576,576]{2,1,0:T(8,128)(2,1)S(1)}, bf16[1,576,576]{2,1,0:T(8,128)(2,1)}, u32[]{:S(2)}) copy-start(bf16[1,576,576]{2,1,0:T(8,128)(2,1)} %param.10) | copy-start | bytes 1990660
  7.2 114.6 %reduce-scatter.8.cloned.1.call-start = ((), (), s32[]{:S(2)}) async-start(), calls=%async_computation.4 | async-start | bytes 1990656 | tf_op jit(solution)/shard_map/reduce_scatter | solution.py:26
  70.0 1.3 copy-start.3
  74.0 64.2 %copy-start.4 = (bf16[1,576,576]{2,1,0:T(8,128)(2,1)S(1)}, bf16[1,576,576]{2,1,0:T(8,128)(2,1)}, u32[]{:S(2)}) copy-start(bf16[1,576,576]{2,1,0:T(8,128)(2,1)} %param.11) | copy-start | bytes 1990660
  74.1 386.2 %all-reduce.8.cloned.1.call-start = ((), (), s32[]{:S(2)}) async-start(), calls=%async_computation.1 | async-start | bytes 786432 | tf_op jit(solution)/shard_map/psum | solution.py:50
  138.8 140.3 %copy-start.5 = (bf16[1,576,256]{2,1,0:T(8,128)(2,1)S(1)}, bf16[1,576,256]{2,1,0:T(8,128)(2,1)}, u32[]{:S(2)}) copy-start(bf16[1,576,256]{2,1,0:T(8,128)(2,1)} %param.12) | copy-start | bytes 884740
  197.9 21.9 %collective-permute-start = (bf16[16,576]{1,0:T(8,128)(2,1)S(1)}, bf16[16,576]{1,0:T(8,128)(2,1)S(1)}, u32[]{:S(2)}, u32[]{:S(2)}) collective-permute-start(bf16[16,576]{1,0:T(8,128)(2,1)S(1)} %convert.14), channel_id=1, source_target_pairs={{0,1},{1,2},{2,3},{3,4},{4,5},{5,6},{6,7},{7,8},{8,9},{9,10},{10,1... | collective-permute-start | bytes 55304
  199.6 23.6 %collective-permute-start.1 = (bf16[16,576]{1,0:T(8,128)(2,1)S(1)}, bf16[16,576]{1,0:T(8,128)(2,1)S(1)}, u32[]{:S(2)}, u32[]{:S(2)}) collective-permute-start(bf16[16,576]{1,0:T(8,128)(2,1)S(1)} %convert.14), channel_id=1, source_target_pairs={{0,2},{1,3},{2,4},{3,5},{4,6},{5,7},{6,8},{7,9},{8,10},{9,11},{10,... | collective-permute-start | bytes 55304
  201.7 15.9 %collective-permute-start.7 = (bf16[12,576]{1,0:T(8,128)(2,1)S(1)}, bf16[12,576]{1,0:T(8,128)(2,1)S(1)}, u32[]{:S(2)}, u32[]{:S(2)}) collective-permute-start(bf16[12,576]{1,0:T(8,128)(2,1)S(1)} %slice.10), channel_id=1, source_target_pairs={{0,8},{1,9},{2,10},{3,11},{4,12},{5,13},{6,14},{7,15},{8,16},{9,17... | collective-permute-start | bytes 41480
  207.7 20.3 %collective-permute-start.2 = (bf16[16,576]{1,0:T(8,128)(2,1)S(1)}, bf16[16,576]{1,0:T(8,128)(2,1)S(1)}, u32[]{:S(2)}, u32[]{:S(2)}) collective-permute-start(bf16[16,576]{1,0:T(8,128)(2,1)S(1)} %convert.14), channel_id=1, source_target_pairs={{0,3},{1,4},{2,5},{3,6},{4,7},{5,8},{6,9},{7,10},{8,11},{9,12},{10... | collective-permute-start | bytes 55304
  212.7 15.3 %collective-permute-start.3 = (bf16[16,576]{1,0:T(8,128)(2,1)S(1)}, bf16[16,576]{1,0:T(8,128)(2,1)S(1)}, u32[]{:S(2)}, u32[]{:S(2)}) collective-permute-start(bf16[16,576]{1,0:T(8,128)(2,1)S(1)} %convert.14), channel_id=1, source_target_pairs={{0,4},{1,5},{2,6},{3,7},{4,8},{5,9},{6,10},{7,11},{8,12},{9,13},{1... | collective-permute-start | bytes 55304
  217.6 10.4 %collective-permute-start.4 = (bf16[16,576]{1,0:T(8,128)(2,1)S(1)}, bf16[16,576]{1,0:T(8,128)(2,1)S(1)}, u32[]{:S(2)}, u32[]{:S(2)}) collective-permute-start(bf16[16,576]{1,0:T(8,128)(2,1)S(1)} %convert.14), channel_id=1, source_target_pairs={{0,5},{1,6},{2,7},{3,8},{4,9},{5,10},{6,11},{7,12},{8,13},{9,14},{... | collective-permute-start | bytes 55304
  219.8 8.3 %collective-permute-start.5 = (bf16[16,576]{1,0:T(8,128)(2,1)S(1)}, bf16[16,576]{1,0:T(8,128)(2,1)S(1)}, u32[]{:S(2)}, u32[]{:S(2)}) collective-permute-start(bf16[16,576]{1,0:T(8,128)(2,1)S(1)} %convert.14), channel_id=1, source_target_pairs={{0,6},{1,7},{2,8},{3,9},{4,10},{5,11},{6,12},{7,13},{8,14},{9,15},... | collective-permute-start | bytes 55304
  223.2 4.8 collective-permute-start.6
  229.4 230.8 %copy-start.2 = (bf16[256,1,576]{0,2,1:T(8,128)(2,1)S(1)}, bf16[256,1,576]{0,2,1:T(8,128)(2,1)}, u32[]{:S(2)}) copy-start(bf16[256,1,576]{0,2,1:T(8,128)(2,1)} %param.14) | copy-start | bytes 884740
  229.4 230.8 %copy-start.6 = (f32[256]{0:T(256)S(1)}, f32[256]{0:T(256)}, u32[]{:S(2)}) copy-start(f32[256]{0:T(256)} %param.13) | copy-start | bytes 3076
  280.2 269.0 %copy-start.7 = (f32[1,576]{1,0:T(1,128)S(1)}, f32[1,576]{1,0:T(1,128)}, u32[]{:S(2)}) copy-start(f32[1,576]{1,0:T(1,128)} %param.15) | copy-start | bytes 6916
  280.2 422.0 %all-reduce.10.cloned.1.call-start = ((), (), s32[]{:S(2)}) async-start(), calls=%async_computation.2 | async-start | bytes 786432 | tf_op jit(solution)/shard_map/psum | solution.py:65
  520.7 23.1 %collective-permute-start.10 = (f32[16,576]{1,0:T(8,128)S(1)}, f32[16,576]{1,0:T(8,128)S(1)}, u32[]{:S(2)}, u32[]{:S(2)}) collective-permute-start(f32[16,576]{1,0:T(8,128)S(1)} %fusion.1), channel_id=1, source_target_pairs={{0,3},{1,4},{2,5},{3,6},{4,7},{5,8},{6,9},{7,10},{8,11},{9,12},{10... | collective-permute-start | bytes 110600
  522.0 24.9 %collective-permute-start.11 = (f32[16,576]{1,0:T(8,128)S(1)}, f32[16,576]{1,0:T(8,128)S(1)}, u32[]{:S(2)}, u32[]{:S(2)}) collective-permute-start(f32[16,576]{1,0:T(8,128)S(1)} %fusion.1), channel_id=1, source_target_pairs={{0,4},{1,5},{2,6},{3,7},{4,8},{5,9},{6,10},{7,11},{8,12},{9,13},{1... | collective-permute-start | bytes 110600
  525.5 15.5 %collective-permute-start.15 = (f32[12,576]{1,0:T(8,128)S(1)}, f32[12,576]{1,0:T(8,128)S(1)}, u32[]{:S(2)}, u32[]{:S(2)}) collective-permute-start(f32[12,576]{1,0:T(8,128)S(1)} %slice.11), channel_id=1, source_target_pairs={{0,8},{1,9},{2,10},{3,11},{4,12},{5,13},{6,14},{7,15},{8,16},{9,17... | collective-permute-start | bytes 82952
  532.6 16.7 %collective-permute-start.12 = (f32[16,576]{1,0:T(8,128)S(1)}, f32[16,576]{1,0:T(8,128)S(1)}, u32[]{:S(2)}, u32[]{:S(2)}) collective-permute-start(f32[16,576]{1,0:T(8,128)S(1)} %fusion.1), channel_id=1, source_target_pairs={{0,5},{1,6},{2,7},{3,8},{4,9},{5,10},{6,11},{7,12},{8,13},{9,14},{... | collective-permute-start | bytes 110600
  537.1 12.2 %collective-permute-start.13 = (f32[16,576]{1,0:T(8,128)S(1)}, f32[16,576]{1,0:T(8,128)S(1)}, u32[]{:S(2)}, u32[]{:S(2)}) collective-permute-start(f32[16,576]{1,0:T(8,128)S(1)} %fusion.1), channel_id=1, source_target_pairs={{0,6},{1,7},{2,8},{3,9},{4,10},{5,11},{6,12},{7,13},{8,14},{9,15},... | collective-permute-start | bytes 110600
  541.0 8.2 %collective-permute-start.14 = (f32[16,576]{1,0:T(8,128)S(1)}, f32[16,576]{1,0:T(8,128)S(1)}, u32[]{:S(2)}, u32[]{:S(2)}) collective-permute-start(f32[16,576]{1,0:T(8,128)S(1)} %fusion.1), channel_id=1, source_target_pairs={{0,7},{1,8},{2,9},{3,10},{4,11},{5,12},{6,13},{7,14},{8,15},{9,16}... | collective-permute-start | bytes 110600
  543.9 5.4 collective-permute-start.8
  547.0 3.3 collective-permute-start.9
  551.3 151.5 %copy-start.1 = (f32[384,256]{1,0:T(8,128)S(1)}, f32[384,256]{1,0:T(8,128)}, u32[]{:S(2)}) copy-start(f32[384,256]{1,0:T(8,128)} %all-reduce.8.cloned.1.call-done) | copy-start | bytes 1179652
  601.5 153.4 %all-reduce.12.cloned.1.call-start = ((), (), s32[]{:S(2)}) async-start(), calls=%async_computation.3 | async-start | bytes 786432 | tf_op jit(solution)/shard_map/psum | solution.py:64
Sparse Core Ops, SparseCore 0:
  74.2 47.5 reduce-scatter.7
  280.3 179.8 all-reduce.7
  601.6 100.4 all-reduce.9
  704.9 49.9 all-reduce.11
